TPU v7x, 32 devices: a whole 2x2x4 slice. The times are simulated.
32 devices in a mesh: rows: 4 (over y, core), cols: 8 (over z, x).
Axes of the slice: x: 2, y: 2, z: 4, core: 2. Of those that a mesh axis runs over, the one named last changes fastest.
Arguments:
- image: bfloat16 [128, 512, 128], P('rows', 'cols'), may hold values from -6 to 6
- routes: int32 [16, 64, 4], P('rows', 'cols'), may hold values from 0 to 1023, as said below
- norm_gain: float32 [128], replicated, may hold values from 0.1 to 1.9
- qkv_weight: bfloat16 [128, 384], replicated, may hold values from -25.455844 to 25.455844
- lce_weight: float32 [5, 5, 128], replicated, may hold values from -1.25 to 1.25
- out_weight: bfloat16 [128, 128], replicated, may hold values from -0.5 to 0.5
- mlp_gain: float32 [128], replicated, may hold values from 0.1 to 1.9
- up_weight: bfloat16 [128, 384], replicated, may hold values from -0.5 to 0.5
- down_weight: bfloat16 [384, 128], replicated, may hold values from -0.3125 to 0.3125
Outputs:
- refined: bfloat16 [128, 512, 128], P('rows', 'cols')
Inputs may be any that keep to these rules, and one draw needn't show every extreme that they name: Each region names 4 different regions. Of the routes of the regions of one device, at most 8 lead to the regions of any one device, and in every draw some device receives exactly 8 from every device.
All inputs are finite; a program needn't handle non-finite values.
Results may differ from a plain program's by a relative error of at most 0.0038.
The roundings to bfloat16 on the way count: a program that leaves them out, or rounds other values in their place, can miss the bound.
Values may be sent and summed in bfloat16 or wider, within the bound.
No kernel may reach another device: no remote copies, remote signals or barrier semaphores. Data moves between devices by JAX's collectives and lax.ppermute only.
A program may use at most 128 MiB of HBM per device.

v0:
```python
import math

import jax
import jax.numpy as jnp
from jax import lax
from jax.sharding import PartitionSpec as P

HEADS = 4


EPSILON = 1e-06


def padded_2(block, sides, width):
    for axis, dim in sides:
        count = lax.axis_size(axis)
        forward = [(i, i + 1) for i in range(count - 1)]
        backward = [(target, source) for source, target in forward]
        low = lax.ppermute(
            lax.slice_in_dim(block, block.shape[dim] - width, None, axis=dim), axis, forward
        )
        high = lax.ppermute(lax.slice_in_dim(block, 0, width, axis=dim), axis, backward)
        block = jnp.concatenate([low, block, high], axis=dim)
    return block


def layer_norm(values, norm_scale):
    floats = values.astype(jnp.float32)
    centered = floats - jnp.mean(floats, axis=-1, keepdims=True)
    spread = jnp.mean(centered * centered, axis=-1, keepdims=True)
    return centered * lax.rsqrt(spread + EPSILON) * norm_scale


def to_regions(grid_field, region_side):
    height, grid_width, channels = grid_field.shape
    shaped = grid_field.reshape(
        height // region_side, region_side, grid_width // region_side, region_side, channels
    )
    return shaped.transpose(0, 2, 1, 3, 4).reshape(-1, region_side * region_side, channels)


def from_regions(blocks, region_side, height, grid_width):
    channels = blocks.shape[-1]
    shaped = blocks.reshape(
        height // region_side, grid_width // region_side, region_side, region_side, channels
    )
    return shaped.transpose(0, 2, 1, 3, 4).reshape(height, grid_width, channels)


def region_attention(queries, keyvals, head_count):
    group_count, length, channels = queries.shape
    head_size = channels // head_count
    q_heads = queries.reshape(group_count, length, head_count, head_size)
    k_heads = keyvals[..., :channels].reshape(group_count, -1, head_count, head_size)
    v_heads = keyvals[..., channels:].reshape(group_count, -1, head_count, head_size)
    scores = jnp.einsum(
        "gqhd,gkhd->ghqk", q_heads, k_heads, preferred_element_type=jnp.float32
    ) * head_size ** (-0.5)
    row_max = jnp.max(scores, axis=-1, keepdims=True)
    expons = jnp.exp(scores - row_max)
    weights = (expons / jnp.sum(expons, axis=-1, keepdims=True)).astype(jnp.bfloat16)
    blended = jnp.einsum("ghqk,gkhd->gqhd", weights, v_heads, preferred_element_type=jnp.float32)
    return blended.reshape(group_count, length, channels)


def local_context(padded, kernel, height, grid_width):
    kernel_size = kernel.shape[0]
    summed = jnp.zeros((height, grid_width, padded.shape[-1]), jnp.float32)
    for offset_row in range(kernel_size):
        for offset_col in range(kernel_size):
            window = padded[
                offset_row : offset_row + height, offset_col : offset_col + grid_width
            ].astype(jnp.float32)
            summed = summed + window * kernel[offset_row, offset_col]
    return summed


def body(
    image, routes, norm_gain, qkv_weight, lce_weight, out_weight, mlp_gain, up_weight, down_weight
):
    height, grid_width, channels = image.shape
    row_devices = lax.axis_size("rows")
    col_devices = lax.axis_size("cols")
    devices = row_devices * col_devices
    region_rows, region_cols, pick_count = routes.shape
    region_side = height // region_rows
    region_count = region_rows * region_cols
    region_area = region_side * region_side
    pair_count = region_count * pick_count
    capacity = max(2, 2 * pair_count // devices)
    all_cols = region_cols * col_devices
    normed = layer_norm(image, norm_gain).astype(jnp.bfloat16)
    projected = jnp.dot(
        normed.reshape(-1, channels), qkv_weight, preferred_element_type=jnp.float32
    )
    projected = projected.astype(jnp.bfloat16).reshape(height, grid_width, 3 * channels)
    queries = to_regions(projected[..., :channels], region_side)
    keyvals = to_regions(projected[..., channels:], region_side)
    values = projected[..., 2 * channels :]
    targets = routes.reshape(pair_count)
    target_row = targets // all_cols
    target_col = targets % all_cols
    owners = target_row // region_rows * col_devices + target_col // region_cols
    local_index = target_row % region_rows * region_cols + target_col % region_cols
    one_hot = (owners[:, None] == jnp.arange(devices, dtype=jnp.int32)[None, :]).astype(jnp.int32)
    before = jnp.cumsum(one_hot, axis=0) - one_hot
    slot_index = jnp.sum(before * one_hot, axis=1)
    position = owners * capacity + slot_index
    requests = jnp.zeros((devices * capacity,), jnp.int32).at[position].set(local_index)
    requested = lax.all_to_all(
        requests.reshape(devices, capacity),
        ("rows", "cols"),
        split_axis=0,
        concat_axis=0,
        tiled=True,
    )
    served = keyvals[requested.reshape(-1)].reshape(devices, capacity, region_area, 2 * channels)
    returned = lax.all_to_all(served, ("rows", "cols"), split_axis=0, concat_axis=0, tiled=True)
    margin = (lce_weight.shape[0] - 1) // 2
    padded = padded_2(values, (("rows", 0), ("cols", 1)), margin)
    context = local_context(padded, lce_weight, height, grid_width)
    fetched = returned.reshape(devices * capacity, region_area, 2 * channels)[position]
    fetched = fetched.reshape(region_count, pick_count * region_area, 2 * channels)
    group_size = math.gcd(region_count, 8)
    group_count = region_count // group_size

    def attend(inputs):
        return region_attention(inputs[0], inputs[1], HEADS)

    blended = lax.map(
        attend,
        (
            queries.reshape(group_count, group_size, region_area, channels),
            fetched.reshape(group_count, group_size, pick_count * region_area, 2 * channels),
        ),
    )
    attended = from_regions(
        blended.reshape(region_count, region_area, channels), region_side, height, grid_width
    )
    combined = (attended + context).astype(jnp.bfloat16)
    projected_out = jnp.dot(
        combined.reshape(-1, channels), out_weight, preferred_element_type=jnp.float32
    )
    residual = image.astype(jnp.float32) + projected_out.reshape(height, grid_width, channels)
    stored = lax.optimization_barrier(residual.astype(jnp.bfloat16))
    second = layer_norm(stored, mlp_gain).astype(jnp.bfloat16)
    hidden = jax.nn.gelu(
        jnp.dot(second.reshape(-1, channels), up_weight, preferred_element_type=jnp.float32),
        approximate=True,
    ).astype(jnp.bfloat16)
    lowered = jnp.dot(hidden, down_weight, preferred_element_type=jnp.float32).reshape(
        height, grid_width, channels
    )
    return (stored.astype(jnp.float32) + lowered).astype(jnp.bfloat16)


def solution(mesh):
    in_specs = (P("rows", "cols", None), P("rows", "cols", None), P(), P(), P(), P(), P(), P(), P())
    out_specs = P("rows", "cols", None)
    return jax.shard_map(body, mesh=mesh, in_specs=in_specs, out_specs=out_specs, check_vma=False)
```

profile of v0, /device:TPU:17, one launch (start us, length us, event | category | flops | bytes accessed | tf_op | source)
XLA Modules:
  0.0 261.6 jit_solution(1552642911192791225)
XLA Ops:
  0.0 0.8 copy.28
  1.6 1.0 scatter_custom_fusion
  2.5 0.7 all_to_all.9
  3.2 6.2 %all-to-all-start = ((s32[32,1,8]{2,1,0:T(1,128)}), s32[32,1,8]{2,1,0:T(1,128)S(1)}, u32[]{:S(2)}, u32[]{:S(2)}) async-start(s32[32,1,8]{2,1,0:T(1,128)} %bitcast.13), calls=%async_computation | async-start | bytes 32768 | tf_op jit(solution)/shard_map/all_to_all | solution.py:110
  9.5 1.4 convert_reduce_fusion.1
  10.9 1.7 fusion.24
  12.6 1.7 fusion.26
  15.5 0.7 reduce.3
  16.3 8.4 %gather_fusion = bf16[256,64,256]{2,1,0:T(8,128)(2,1)} fusion(bf16[32,64,256]{2,1,0:T(8,128)(2,1)S(1)} %bitcast.114, s32[1024]{0:T(1024)S(1)} %pad_clamp_fusion.1), kind=kCustom, calls=%fused_computation | custom fusion | bytes 16778240 | tf_op jit(solution)/shard_map/gather | solution.py:117
  24.8 5.9 %all-to-all-start.1 = ((bf16[32,8,64,256]{3,2,1,0:T(8,128)(2,1)}), bf16[32,8,64,256]{3,2,1,0:T(8,128)(2,1)}, u32[]{:S(2)}, u32[]{:S(2)}) async-start(bf16[32,8,64,256]{3,2,1,0:T(8,128)(2,1)} %bitcast.116), calls=%async_computation.1 | async-start | bytes 16777216 | tf_op jit(solution)/shard_map/all_to_all | solution.py:118
  30.7 3.4 %collective-permute-start = (bf16[2,64,128]{2,1,0:T(8,128)(2,1)S(1)}, bf16[2,64,128]{2,1,0:T(8,128)(2,1)S(1)}, u32[]{:S(2)}, u32[]{:S(2)}) collective-permute-start(bf16[2,64,128]{2,1,0:T(8,128)(2,1)S(1)} %get-tuple-element.56), channel_id=1, source_target_pairs={{0,8},{8,16},{16,24},{1,9},{9,17},{17,25},{2,10},{10,18},{18,26},{... | collective-permute-start | bytes 98312 | tf_op jit(solution)/shard_map/ppermute | solution.py:19
  34.1 1.9 collective-permute-start.1
  36.0 0.7 slice_bitcast_fusion.24
  37.0 0.7 slice_bitcast_fusion.23
  37.6 33.3 %collective-permute-done = bf16[2,64,128]{2,1,0:T(8,128)(2,1)S(1)} collective-permute-done((bf16[2,64,128]{2,1,0:T(8,128)(2,1)S(1)}, bf16[2,64,128]{2,1,0:T(8,128)(2,1)S(1)}, u32[]{:S(2)}, u32[]{:S(2)}) %collective-permute-start) | collective-permute-done | bytes 32800 | tf_op jit(solution)/shard_map/ppermute | solution.py:19
  71.0 7.5 %collective-permute-done.1 = bf16[2,64,128]{2,1,0:T(8,128)(2,1)S(1)} collective-permute-done((bf16[2,64,128]{2,1,0:T(8,128)(2,1)S(1)}, bf16[2,64,128]{2,1,0:T(8,128)(2,1)S(1)}, u32[]{:S(2)}, u32[]{:S(2)}) %collective-permute-start.1) | collective-permute-done | bytes 32800 | tf_op jit(solution)/shard_map/ppermute | solution.py:22
  78.5 1.9 collective-permute-start.2
  80.4 4.4 %collective-permute-start.3 = (bf16[36,2,128]{2,1,0:T(2,128)(2,1)S(1)}, bf16[36,2,128]{2,1,0:T(2,128)(2,1)S(1)}, u32[]{:S(2)}, u32[]{:S(2)}) collective-permute-start(bf16[36,2,128]{2,1,0:T(2,128)(2,1)S(1)} %get-tuple-element.63), channel_id=1, source_target_pairs={{1,0},{2,1},{3,2},{4,3},{5,4},{6,5},{7,6},{9,8},{10,9},{11,10},{12... | collective-permute-start | bytes 55304 | tf_op jit(solution)/shard_map/ppermute | solution.py:22
  84.9 0.9 copy.45
  85.8 131.1 %collective-permute-done.2 = bf16[36,2,128]{2,1,0:T(2,128)(2,1)S(1)} collective-permute-done((bf16[36,2,128]{2,1,0:T(2,128)(2,1)S(1)}, bf16[36,2,128]{2,1,0:T(2,128)(2,1)S(1)}, u32[]{:S(2)}, u32[]{:S(2)}) %collective-permute-start.2) | collective-permute-done | bytes 18464 | tf_op jit(solution)/shard_map/ppermute | solution.py:19
  216.9 1.4 maximum_maximum_fusion
  218.4 6.2 %gather_fusion.1 = bf16[128,64,256]{2,1,0:T(8,128)(2,1)} fusion(bf16[256,64,256]{2,1,0:T(8,128)(2,1)} %bitcast.16, s32[1024]{0:T(1024)S(1)} %pad_clamp_fusion), kind=kCustom, calls=%fused_computation.1 | custom fusion | bytes 8389120 | tf_op jit(solution)/shard_map/gather | solution.py:122
  224.5 22.9 %while.10 = (s32[]{:T(128)}, f32[4,8,64,128]{3,2,1,0:T(8,128)}, bf16[4,8,256,256]{3,2,1,0:T(8,128)(2,1)}, bf16[4,8,64,128]{3,2,1,0:T(8,128)(2,1)}, s32[]{:T(128)}) while((s32[]{:T(128)}, f32[4,8,64,128]{3,2,1,0:T(8,128)}, bf16[4,8,256,256]{3,2,1,0:T(8,128)(2,1)}, bf16[4,8,64,128]{3,2,1,0:T(8,128)(2,1)}, s32[]{:T(128)}) %tuple.60), condition=%wide.region_8.9_spmd, body=%wide.region_5.8_spmd.sunk | while | flops 69730560 | bytes 13517381 | solution.py:130
  224.5 1.3 constant_dynamic-slice_fusion.4
  226.5 0.9 constant_dynamic-slice_fusion.5
  227.6 1.0 fusion.64
  228.6 0.7 fusion.65
  229.5 0.7 constant_dynamic-update-slice_fusion.2
  230.3 1.3 constant_dynamic-slice_fusion.4
  232.2 0.9 constant_dynamic-slice_fusion.5
  233.3 1.0 fusion.64
  234.3 0.7 fusion.65
  235.2 0.7 constant_dynamic-update-slice_fusion.2
  236.0 1.3 constant_dynamic-slice_fusion.4
  237.9 0.9 constant_dynamic-slice_fusion.5
  239.0 1.0 fusion.64
  240.0 0.7 fusion.65
  241.0 0.7 constant_dynamic-update-slice_fusion.2
  241.7 1.3 constant_dynamic-slice_fusion.4
  243.6 0.9 constant_dynamic-slice_fusion.5
  244.7 1.0 fusion.64
  245.7 0.7 fusion.65
  246.7 0.7 constant_dynamic-update-slice_fusion.2
  247.7 1.5 copy.35
  249.5 8.2 %fusion.16 = bf16[32,64,128]{2,1,0:T(8,128)(2,1)S(1)} fusion(bf16[32,64,128]{2,1,0:T(8,128)(2,1)S(1)} %copy-done.1, f32[32,64,128]{2,1,0:T(8,128)S(1)} %bitcast.127, bf16[32,64,128]{2,1,0:T(8,128)(2,1)S(1)} %copy-done.3, bf16[2,64,128]{2,1,0:T(8,128)(2,1)S(1)} %copy-done.6, bf16[2,64,128]{2,1,0:T(8,128)(2,1)S(1)} %collective-permute-done, ...), kind=kOutput, calls=%fused_computation.32 | convolution fusion | flops 88866816 | bytes 13218304 | tf_op jit(solution)/shard_map/dot_general | solution.py:141
  258.0 0.6 fusion.21
  259.3 1.3 fusion.15
  260.6 0.9 fusion.27
  (119 shorter events, 7.5 us)
Async XLA Ops:
  0.0 14.2 %copy-start = (bf16[128,384]{1,0:T(8,128)(2,1)S(1)}, bf16[128,384]{1,0:T(8,128)(2,1)}, u32[]{:S(2)}) copy-start(bf16[128,384]{1,0:T(8,128)(2,1)} %param.14) | copy-start | bytes 294916
  3.2 11.8 %all-to-all-start = ((s32[32,1,8]{2,1,0:T(1,128)}), s32[32,1,8]{2,1,0:T(1,128)S(1)}, u32[]{:S(2)}, u32[]{:S(2)}) async-start(s32[32,1,8]{2,1,0:T(1,128)} %bitcast.13), calls=%async_computation | async-start | bytes 32768 | tf_op jit(solution)/shard_map/all_to_all | solution.py:110
  24.8 11.2 %copy-start.7 = (f32[5,5,128]{2,1,0:T(8,128)S(1)}, f32[5,5,128]{2,1,0:T(8,128)}, u32[]{:S(2)}) copy-start(f32[5,5,128]{2,1,0:T(8,128)} %param.15) | copy-start | bytes 38404
  24.8 193.6 %all-to-all-start.1 = ((bf16[32,8,64,256]{3,2,1,0:T(8,128)(2,1)}), bf16[32,8,64,256]{3,2,1,0:T(8,128)(2,1)}, u32[]{:S(2)}, u32[]{:S(2)}) async-start(bf16[32,8,64,256]{3,2,1,0:T(8,128)(2,1)} %bitcast.116), calls=%async_computation.1 | async-start | bytes 16777216 | tf_op jit(solution)/shard_map/all_to_all | solution.py:118
  30.7 40.3 %collective-permute-start = (bf16[2,64,128]{2,1,0:T(8,128)(2,1)S(1)}, bf16[2,64,128]{2,1,0:T(8,128)(2,1)S(1)}, u32[]{:S(2)}, u32[]{:S(2)}) collective-permute-start(bf16[2,64,128]{2,1,0:T(8,128)(2,1)S(1)} %get-tuple-element.56), channel_id=1, source_target_pairs={{0,8},{8,16},{16,24},{1,9},{9,17},{17,25},{2,10},{10,18},{18,26},{... | collective-permute-start | bytes 98312 | tf_op jit(solution)/shard_map/ppermute | solution.py:19
  34.1 44.4 %collective-permute-start.1 = (bf16[2,64,128]{2,1,0:T(8,128)(2,1)S(1)}, bf16[2,64,128]{2,1,0:T(8,128)(2,1)S(1)}, u32[]{:S(2)}, u32[]{:S(2)}) collective-permute-start(bf16[2,64,128]{2,1,0:T(8,128)(2,1)S(1)} %get-tuple-element.57), channel_id=1, source_target_pairs={{8,0},{16,8},{24,16},{9,1},{17,9},{25,17},{10,2},{18,10},{26,18},{... | collective-permute-start | bytes 98312 | tf_op jit(solution)/shard_map/ppermute | solution.py:22
  37.0 187.6 %copy-start.2 = (bf16[32,64,128]{2,1,0:T(8,128)(2,1)}, bf16[32,64,128]{2,1,0:T(8,128)(2,1)S(1)}, u32[]{:S(2)}) copy-start(bf16[32,64,128]{2,1,0:T(8,128)(2,1)S(1)} %get-tuple-element.58) | copy-start | bytes 1572868
  78.4 146.1 %copy-start.5 = (bf16[2,64,128]{2,1,0:T(8,128)(2,1)}, bf16[2,64,128]{2,1,0:T(8,128)(2,1)S(1)}, u32[]{:S(2)}) copy-start(bf16[2,64,128]{2,1,0:T(8,128)(2,1)S(1)} %collective-permute-done.1) | copy-start | bytes 98308
  78.5 138.4 %collective-permute-start.2 = (bf16[36,2,128]{2,1,0:T(2,128)(2,1)S(1)}, bf16[36,2,128]{2,1,0:T(2,128)(2,1)S(1)}, u32[]{:S(2)}, u32[]{:S(2)}) collective-permute-start(bf16[36,2,128]{2,1,0:T(2,128)(2,1)S(1)} %get-tuple-element.62), channel_id=1, source_target_pairs={{0,1},{1,2},{2,3},{3,4},{4,5},{5,6},{6,7},{8,9},{9,10},{10,11},{11... | collective-permute-start | bytes 55304 | tf_op jit(solution)/shard_map/ppermute | solution.py:19
  80.4 136.5 %collective-permute-start.3 = (bf16[36,2,128]{2,1,0:T(2,128)(2,1)S(1)}, bf16[36,2,128]{2,1,0:T(2,128)(2,1)S(1)}, u32[]{:S(2)}, u32[]{:S(2)}) collective-permute-start(bf16[36,2,128]{2,1,0:T(2,128)(2,1)S(1)} %get-tuple-element.63), channel_id=1, source_target_pairs={{1,0},{2,1},{3,2},{4,3},{5,4},{6,5},{7,6},{9,8},{10,9},{11,10},{12... | collective-permute-start | bytes 55304 | tf_op jit(solution)/shard_map/ppermute | solution.py:22
  247.4 1.8 copy-start.1
  247.4 1.8 copy-start.3
  247.4 1.8 copy-start.4
  247.4 1.8 copy-start.6
  247.4 1.8 copy-start.9
  247.4 1.8 copy-start.10
  247.4 1.8 copy-start.11
  247.4 1.8 copy-start.12
  247.5 1.8 copy-start.13
  247.5 1.8 copy-start.14
  247.5 1.8 copy-start.15
  247.5 1.8 copy-start.16
  247.5 1.8 copy-start.17
  247.5 1.8 copy-start.18
  247.5 1.8 copy-start.19
  247.5 1.8 copy-start.20
  247.5 1.8 copy-start.21
  247.5 1.8 copy-start.22
  247.6 1.8 copy-start.23
  247.6 1.8 copy-start.24
  247.6 1.8 copy-start.25
  247.6 1.8 copy-start.26
  247.6 1.8 copy-start.27
  247.6 1.8 copy-start.28
  247.6 1.8 copy-start.29
  247.6 1.8 copy-start.30
  247.6 1.8 copy-start.31
  247.6 1.8 copy-start.32
  247.7 1.8 copy-start.33
  247.7 1.8 copy-start.36
  249.5 9.2 %copy-start.8 = (f32[128]{0:T(128)S(1)}, f32[128]{0:T(128)}, u32[]{:S(2)}) copy-start(f32[128]{0:T(128)} %param.17) | copy-start | bytes 1540
  257.6 1.7 copy-start.34
  257.7 1.7 copy-start.35
where the time goes:
time: 262 us
  waiting for transfers between devices  172 us (66%)
  local copies, waits for them, and re-layouts  37.9 us (14%)
  starting transfers between devices  23.8 us (9%)
  matrix products  17.1 us (7%)
  other arithmetic  9.96 us (4%)
    ppermute x2, waiting for transfers between devices, padded_2(): lax.ppermute(lax.slice_in_dim(block, block.shape[dim] - width, None, axis...  164 us
    dynamic_slice x16, local copies, waits for them, and re-layouts, body(): lax.map(attend, (queries.reshape(group_count, group_size, region_area, ch...  11.7 us
    gather x1, local copies, waits for them, and re-layouts, body(): keyvals[requested.reshape(-1)]  8.41 us
    dot_general x1, matrix products, body(): jnp.dot(combined.reshape(-1, channels), out_weight, preferred_element_typ...  8.16 us
    ppermute x2, waiting for transfers between devices, padded_2(): lax.ppermute(lax.slice_in_dim(block, 0, width, axis=dim), axis, backward)  7.5 us
    ppermute x2, starting transfers between devices, padded_2(): lax.ppermute(lax.slice_in_dim(block, 0, width, axis=dim), axis, backward)  6.36 us
    all_to_all x1, starting transfers between devices, body(): lax.all_to_all(requests.reshape(devices, capacity), ('rows', 'cols'), spl...  6.22 us
    gather x1, local copies, waits for them, and re-layouts, body(): returned.reshape(devices * capacity, region_area, 2 * channels)[position]  6.17 us
  transfers between devices with their start and end apart: 6, of which 3 were waited for; matrix products, arithmetic and copies ran while one was open for 4% of the time, Pallas kernels for 0%

commit v1 on v0

v1 whole, which is shorter than its diff:
```python
import functools
import math

import jax
import jax.numpy as jnp
from jax import lax
from jax.experimental import pallas as pl
from jax.experimental.pallas import tpu as pltpu
from jax.sharding import PartitionSpec as P

HEADS = 4
EPSILON = 1e-06
F32 = jnp.float32
BF16 = jnp.bfloat16


def halo(block, sides, width):
    for axis, dim in sides:
        count = lax.axis_size(axis)
        forward = [(i, i + 1) for i in range(count - 1)]
        backward = [(target, source) for source, target in forward]
        low = lax.ppermute(
            lax.slice_in_dim(block, block.shape[dim] - width, None, axis=dim), axis, forward
        )
        high = lax.ppermute(lax.slice_in_dim(block, 0, width, axis=dim), axis, backward)
        block = jnp.concatenate([low, block, high], axis=dim)
    return block


def normalize(floats, gain):
    centered = floats - jnp.mean(floats, axis=-1, keepdims=True)
    spread = jnp.mean(centered * centered, axis=-1, keepdims=True)
    return centered * lax.rsqrt(spread + EPSILON) * gain


def regions_of(strip, side):
    height, width, channels = strip.shape
    return (
        strip.reshape(height, width // side, side, channels)
        .transpose(1, 0, 2, 3)
        .reshape(height * width, channels)
    )


def strip_of(tokens, side, width):
    channels = tokens.shape[-1]
    return (
        tokens.reshape(width // side, side, side, channels)
        .transpose(1, 0, 2, 3)
        .reshape(side, width, channels)
    )


def norm_kernel(side, image_ref, gain_ref, out_ref):
    normed = normalize(image_ref[...].astype(F32), gain_ref[...])
    out_ref[...] = regions_of(normed, side).astype(BF16).reshape(out_ref.shape)


def norm_regions(image, gain, side):
    height, width, channels = image.shape
    per_row = width // side
    return pl.pallas_call(
        functools.partial(norm_kernel, side),
        grid=(height // side,),
        in_specs=[
            pl.BlockSpec((side, width, channels), lambda i: (i, 0, 0)),
            pl.BlockSpec((1, channels), lambda i: (0, 0)),
        ],
        out_specs=pl.BlockSpec((per_row, side * side, channels), lambda i: (i, 0, 0)),
        out_shape=jax.ShapeDtypeStruct(
            (height // side * per_row, side * side, channels), BF16
        ),
        cost_estimate=pl.CostEstimate(
            flops=10 * image.size, bytes_accessed=4 * image.size, transcendentals=0
        ),
        name="norm_regions",
    )(image, gain.reshape(1, channels))


def context_kernel(side, kernel_size, padded_ref, gain_ref, weight_ref, lce_ref, context_ref, query_ref):
    step = pl.program_id(0)
    rows = side + kernel_size - 1
    channels = padded_ref.shape[-1]
    width = query_ref.shape[0] // side
    strip = padded_ref[pl.ds(step * side, rows)].astype(F32)
    wide = strip.shape[1]
    normed = normalize(strip, gain_ref[...]).astype(BF16).reshape(rows * wide, channels)
    projected = jnp.dot(normed, weight_ref[...], preferred_element_type=F32).astype(BF16)
    values = projected[:, channels:].astype(F32).reshape(rows, wide, channels)
    summed = jnp.zeros((side, width, channels), F32)
    for col in range(kernel_size):
        moved = values if col == 0 else pltpu.roll(values, wide - col, 1)
        moved = moved[:, :width]
        for row in range(kernel_size):
            summed = summed + moved[row : row + side] * lce_ref[row, col]
    context_ref[...] = regions_of(summed, side)
    margin = (kernel_size - 1) // 2
    queries = projected[:, :channels].astype(F32).reshape(rows, wide, channels)
    inner = pltpu.roll(queries, wide - margin, 1)[margin : margin + side, :width]
    query_ref[...] = regions_of(inner, side).astype(BF16)


def context_and_queries(padded, gain, query_value_weight, lce_weight, side, height, width):
    channels = padded.shape[-1]
    kernel_size = lce_weight.shape[0]
    tokens = height * width
    full = lambda shape: pl.BlockSpec(shape, lambda i: (0,) * len(shape))
    return pl.pallas_call(
        functools.partial(context_kernel, side, kernel_size),
        grid=(height // side,),
        in_specs=[
            full(padded.shape),
            full((1, channels)),
            full(query_value_weight.shape),
            full((kernel_size, kernel_size, 1, channels)),
        ],
        out_specs=[
            pl.BlockSpec((side * width, channels), lambda i: (i, 0)),
            pl.BlockSpec((side * width, channels), lambda i: (i, 0)),
        ],
        out_shape=[
            jax.ShapeDtypeStruct((tokens, channels), F32),
            jax.ShapeDtypeStruct((tokens, channels), BF16),
        ],
        cost_estimate=pl.CostEstimate(
            flops=tokens * channels * 600, bytes_accessed=10 * tokens * channels, transcendentals=0
        ),
        name="context",
    )(
        padded,
        gain.reshape(1, channels),
        query_value_weight,
        lce_weight.reshape(kernel_size, kernel_size, 1, channels),
    )


def pack_kernel(index_ref, source_ref, out_ref):
    step = pl.program_id(0)
    count = out_ref.shape[0]

    def one(slot, carry):
        out_ref[slot] = source_ref[index_ref[step * count + slot]]
        return carry

    lax.fori_loop(0, count, one, 0, unroll=True)


def pack(source, index, steps):
    slots = index.shape[0]
    shape = source.shape[1:]
    per_step = slots // steps
    return pl.pallas_call(
        pack_kernel,
        grid_spec=pltpu.PrefetchScalarGridSpec(
            num_scalar_prefetch=1,
            grid=(steps,),
            in_specs=[pl.BlockSpec(source.shape, lambda i, index: (0, 0, 0))],
            out_specs=pl.BlockSpec((per_step, *shape), lambda i, index: (i, 0, 0)),
        ),
        out_shape=jax.ShapeDtypeStruct((slots, *shape), source.dtype),
        cost_estimate=pl.CostEstimate(
            flops=0, bytes_accessed=4 * slots * math.prod(shape), transcendentals=0
        ),
        name="pack",
    )(index, source)


def tail_kernel(side, picks, batch, *refs):
    pieces = refs[1 : 1 + batch * picks]
    (
        query_ref,
        context_ref,
        image_ref,
        key_ref,
        value_ref,
        out_weight_ref,
        gain_ref,
        up_ref,
        down_ref,
        result_ref,
    ) = refs[1 + batch * picks :]
    area, channels = pieces[0].shape
    head_size = channels // HEADS
    lane = lax.broadcasted_iota(jnp.int32, (area, channels), 1) // head_size
    attended = []
    for region in range(batch):
        rows = pl.ds(region * area, area)
        fetched = jnp.concatenate(
            [piece[...] for piece in pieces[region * picks : (region + 1) * picks]], axis=0
        )
        keys = jnp.dot(fetched, key_ref[...], preferred_element_type=F32).astype(BF16)
        values = jnp.dot(fetched, value_ref[...], preferred_element_type=F32).astype(BF16)
        queries = query_ref[rows, :]
        zero = jnp.zeros_like(queries)
        stacked = jnp.concatenate(
            [jnp.where(lane == head, queries, zero) for head in range(HEADS)], axis=0
        )
        scores = lax.dot_general(
            stacked, keys, (((1,), (1,)), ((), ())), preferred_element_type=F32
        ) * head_size ** (-0.5)
        expons = jnp.exp(scores - jnp.max(scores, axis=-1, keepdims=True))
        weights = (expons * (1.0 / jnp.sum(expons, axis=-1, keepdims=True))).astype(BF16)
        blended = jnp.dot(weights, values, preferred_element_type=F32)
        picked = jnp.zeros((area, channels), F32)
        for head in range(HEADS):
            picked = jnp.where(lane == head, blended[head * area : (head + 1) * area], picked)
        attended.append(picked)
    combined = (jnp.concatenate(attended, axis=0) + context_ref[...]).astype(BF16)
    image = regions_of(image_ref[...].astype(F32), side)
    residual = image + jnp.dot(combined, out_weight_ref[...], preferred_element_type=F32)
    stored = residual.astype(BF16).astype(F32)
    second = normalize(stored, gain_ref[...]).astype(BF16)
    lifted = jnp.dot(second, up_ref[...], preferred_element_type=F32)
    hidden = jax.nn.gelu(lifted, approximate=True).astype(BF16)
    refined = stored + jnp.dot(hidden, down_ref[...], preferred_element_type=F32)
    result_ref[...] = strip_of(refined, side, batch * side).astype(BF16)


def tail(position, table, queries, context, image, weights, side, picks):
    height, width, channels = image.shape
    area = side * side
    per_row = width // side
    batch = math.gcd(per_row, 4)
    halves = per_row // batch

    def piece(which):
        return pl.BlockSpec(
            (None, area, channels),
            lambda i, j, position: (
                position[((i * halves + j) * batch) * picks + which],
                0,
                0,
            ),
        )

    full = lambda a: pl.BlockSpec(a.shape, lambda i, j, position: (0,) * a.ndim)
    tokens = pl.BlockSpec((batch * area, channels), lambda i, j, position: (i * halves + j, 0))
    strip = pl.BlockSpec((side, batch * side, channels), lambda i, j, position: (i, j, 0))
    return pl.pallas_call(
        functools.partial(tail_kernel, side, picks, batch),
        grid_spec=pltpu.PrefetchScalarGridSpec(
            num_scalar_prefetch=1,
            grid=(height // side, halves),
            in_specs=[piece(i) for i in range(batch * picks)]
            + [tokens, tokens, strip]
            + [full(w) for w in weights],
            out_specs=strip,
        ),
        out_shape=jax.ShapeDtypeStruct(image.shape, BF16),
        cost_estimate=pl.CostEstimate(
            flops=image.size * 4000, bytes_accessed=16 * image.size, transcendentals=40 * image.size
        ),
        name="tail",
    )(position, *([table] * (batch * picks)), queries, context, image, *weights)


def body(
    image, routes, norm_gain, qkv_weight, lce_weight, out_weight, mlp_gain, up_weight, down_weight
):
    height, grid_width, channels = image.shape
    col_devices = lax.axis_size("cols")
    devices = lax.axis_size("rows") * col_devices
    region_rows, region_cols, pick_count = routes.shape
    side = height // region_rows
    pair_count = region_rows * region_cols * pick_count
    capacity = max(2, 2 * pair_count // devices)
    all_cols = region_cols * col_devices

    targets = routes.reshape(pair_count)
    target_row = targets // all_cols
    target_col = targets % all_cols
    owners = target_row // region_rows * col_devices + target_col // region_cols
    local_index = target_row % region_rows * region_cols + target_col % region_cols
    pairs = jnp.arange(pair_count, dtype=jnp.int32)
    earlier = (owners[:, None] == owners[None, :]) & (pairs[None, :] < pairs[:, None])
    position = owners * capacity + jnp.sum(earlier.astype(jnp.int32), axis=1)
    slots = jnp.arange(devices * capacity, dtype=jnp.int32)
    requests = jnp.sum(
        jnp.where(position[None, :] == slots[:, None], local_index[None, :], 0), axis=1
    )
    requested = lax.all_to_all(
        requests.reshape(devices, capacity), ("rows", "cols"), 0, 0, tiled=True
    )

    normed = norm_regions(image, norm_gain, side)
    served = pack(normed, requested.reshape(-1), math.gcd(devices, 8))
    table = lax.all_to_all(
        served.reshape(devices, capacity, *normed.shape[1:]), ("rows", "cols"), 0, 0, tiled=True
    ).reshape(served.shape)

    margin = (lce_weight.shape[0] - 1) // 2
    padded = halo(image, (("rows", 0), ("cols", 1)), margin)
    padded = jnp.pad(padded, ((0, 0), (0, -padded.shape[1] % 16), (0, 0)))
    query_value = jnp.concatenate(
        [qkv_weight[:, :channels], qkv_weight[:, 2 * channels :]], axis=1
    )
    context, queries = context_and_queries(
        padded, norm_gain, query_value, lce_weight, side, height, grid_width
    )
    weights = (
        qkv_weight[:, channels : 2 * channels],
        qkv_weight[:, 2 * channels :],
        out_weight,
        mlp_gain.reshape(1, channels),
        up_weight,
        down_weight,
    )
    return tail(position, table, queries, context, image, weights, side, pick_count)


def solution(mesh):
    in_specs = (P("rows", "cols", None), P("rows", "cols", None), P(), P(), P(), P(), P(), P(), P())
    out_specs = P("rows", "cols", None)
    return jax.shard_map(body, mesh=mesh, in_specs=in_specs, out_specs=out_specs, check_vma=False)
```

time: 262 us -> 148 us (0.56)
  waiting for transfers between devices: 172 us -> 79.4 us
  Pallas kernels: 0 us -> 36.1 us
  local copies, waits for them, and re-layouts: 37.9 us -> 4.17 us
  matrix products: 17.1 us -> 0 us
  other arithmetic: 9.96 us -> 2.82 us
    ppermute x4, waiting for transfers between devices: 172 us -> 78.2 us  [the longest x2 76.1 us: halo(): lax.ppermute(lax.slice_in_dim(block, block.shape[dim] - width, None, axis...]
    pallas_call x0 -> x4, Pallas kernels: none -> 36.1 us  [the longest x1 21.3 us: tail(): pl.pallas_call(functools.partial(tail_kernel, side, picks, batch), grid_s...]
    gather x2 -> x0, local copies, waits for them, and re-layouts: 14.6 us -> none  [the longest x1 8.41 us: body(): keyvals[requested.reshape(-1)]]
    dot_general x7 -> x0, matrix products: 12.9 us -> none  [the longest x1 8.16 us: body(): jnp.dot(combined.reshape(-1, channels), out_weight, preferred_element_typ...]
    dynamic_slice x16 -> x0, local copies, waits for them, and re-layouts: 11.7 us -> none  [body(): lax.map(attend, (queries.reshape(group_count, group_size, region_area, ch...]
    sub x4 -> x0, matrix products: 4.14 us -> none  [region_attention(): expons = jnp.exp(scores - row_max)]
    reduce_sum x5 -> x2, other arithmetic: 4.23 us -> 0.28 us  [the longest x1 0.17 us: body(): position = owners * capacity + jnp.sum(earlier.astype(jnp.int32), axis=1)]
    dynamic_update_slice x8 -> x0, local copies, waits for them, and re-layouts: 3.62 us -> none  [body(): lax.map(attend, (queries.reshape(group_count, group_size, region_area, ch...]
  transfers between devices with their start and end apart: 6 -> 6, of which waited for: 3 -> 4; matrix products, arithmetic and copies ran while one was open for 4% -> 2% of each run, Pallas kernels for 0% -> 6%
where the time goes in v1:
time: 148 us; the launch traced here: 147 us
  waiting for transfers between devices  79.4 us (54%)
  Pallas kernels  36.1 us (24%)
  starting transfers between devices  24.6 us (17%)
  local copies, waits for them, and re-layouts  4.17 us (3%)
  other arithmetic  2.82 us (2%)
    ppermute x2, waiting for transfers between devices, halo(): lax.ppermute(lax.slice_in_dim(block, block.shape[dim] - width, None, axis...  76.1 us
    pallas_call x1, Pallas kernels, tail(): pl.pallas_call(functools.partial(tail_kernel, side, picks, batch), grid_s...  21.3 us
    ppermute x2, starting transfers between devices, halo(): lax.ppermute(lax.slice_in_dim(block, block.shape[dim] - width, None, axis...  8.61 us
    all_to_all x1, starting transfers between devices, body(): lax.all_to_all(requests.reshape(devices, capacity), ('rows', 'cols'), 0,...  6.22 us
    all_to_all x1, starting transfers between devices, body(): lax.all_to_all(served.reshape(devices, capacity, *normed.shape[1:]), ('ro...  5.95 us
    pallas_call x1, Pallas kernels, context_and_queries(): pl.pallas_call(functools.partial(context_kernel, side, kernel_size), grid...  5.85 us
    pallas_call x1, Pallas kernels, pack(): pl.pallas_call(pack_kernel, grid_spec=pltpu.PrefetchScalarGridSpec(num_sc...  5.35 us
    ppermute x2, starting transfers between devices, halo(): lax.ppermute(lax.slice_in_dim(block, 0, width, axis=dim), axis, backward)  3.84 us
  transfers between devices with their start and end apart: 6, of which 4 were waited for; matrix products, arithmetic and copies ran while one was open for 2% of the time, Pallas kernels for 6%

profile of v1, /device:TPU:17, one launch (start us, length us, event | category | flops | bytes accessed | tf_op | source)
XLA Modules:
  0.0 147.3 jit_solution(6911752764539605800)
XLA Ops:
  0.0 0.8 copy.14
  0.8 0.1 reshape.245
  0.9 0.2 convert_reduce_fusion
  1.1 0.0 copy-start.4
  1.1 0.1 select_reduce_fusion
  1.3 0.7 all_to_all.9
  1.9 6.2 %all-to-all-start = ((s32[32,1,8]{2,1,0:T(1,128)}), s32[32,1,8]{2,1,0:T(1,128)S(1)}, u32[]{:S(2)}, u32[]{:S(2)}) async-start(s32[32,1,8]{2,1,0:T(1,128)} %bitcast), calls=%async_computation | async-start | bytes 32768 | tf_op jit(solution)/shard_map/all_to_all | solution.py:281
  8.2 3.6 %norm_regions.1.source_ref = bf16[32,64,128]{2,1,0:T(8,128)(2,1)} custom-call(bf16[32,64,128]{2,1,0:T(8,128)(2,1)} %refs_19_.1, f32[1,128]{1,0:T(1,128)} %bitcast.6), custom_call_target="tpu_custom_call" | custom-call | flops 2621440 | bytes 1048576 | tf_op jit(solution)/shard_map/norm_regions/pallas_call | solution.py:62
  11.8 1.2 all-to-all-done
  13.0 0.6 broadcast.431
  13.5 0.7 reduce.3
  14.2 0.7 reshape.246.index_ref
  14.9 5.3 %pack.1 = bf16[256,64,128]{2,1,0:T(8,128)(2,1)} custom-call(s32[256]{0:T(256)} %reshape.246.index_ref, bf16[32,64,128]{2,1,0:T(8,128)(2,1)} %norm_regions.1.source_ref), custom_call_target="tpu_custom_call" | custom-call | bytes 8388608 | tf_op jit(solution)/shard_map/pack/pallas_call | solution.py:152
  20.2 0.0 copy-done.4
  20.2 0.0 copy-start
  20.2 0.0 copy-start.2
  20.2 6.0 %all-to-all-start.1 = ((bf16[32,8,64,128]{3,2,1,0:T(8,128)(2,1)}), bf16[32,8,64,128]{3,2,1,0:T(8,128)(2,1)}, u32[]{:S(2)}, u32[]{:S(2)}) async-start(bf16[32,8,64,128]{3,2,1,0:T(8,128)(2,1)} %bitcast.5), calls=%async_computation.1 | async-start | bytes 8388608 | tf_op jit(solution)/shard_map/all_to_all | solution.py:287
  26.2 0.0 copy-done
  26.2 0.0 copy-start.3
  26.2 3.4 %collective-permute-start = (bf16[2,64,128]{2,1,0:T(8,128)(2,1)S(1)}, bf16[2,64,128]{2,1,0:T(8,128)(2,1)S(1)}, u32[]{:S(2)}, u32[]{:S(2)}) collective-permute-start(bf16[2,64,128]{2,1,0:T(8,128)(2,1)S(1)} %get-tuple-element.16), channel_id=1, source_target_pairs={{0,8},{8,16},{16,24},{1,9},{9,17},{17,25},{2,10},{10,18},{18,26},{... | collective-permute-start | bytes 98312 | tf_op jit(solution)/shard_map/ppermute | solution.py:22
  29.6 1.9 %collective-permute-start.1 = (bf16[2,64,128]{2,1,0:T(8,128)(2,1)S(1)}, bf16[2,64,128]{2,1,0:T(8,128)(2,1)S(1)}, u32[]{:S(2)}, u32[]{:S(2)}) collective-permute-start(bf16[2,64,128]{2,1,0:T(8,128)(2,1)S(1)} %get-tuple-element.15), channel_id=1, source_target_pairs={{8,0},{16,8},{24,16},{9,1},{17,9},{25,17},{10,2},{18,10},{26,18},{... | collective-permute-start | bytes 98312 | tf_op jit(solution)/shard_map/ppermute | solution.py:25
  31.6 0.0 copy-done.2
  31.6 0.6 fusion.10
  32.2 0.0 copy-start.1
  32.2 14.6 %collective-permute-done = bf16[2,64,128]{2,1,0:T(8,128)(2,1)S(1)} collective-permute-done((bf16[2,64,128]{2,1,0:T(8,128)(2,1)S(1)}, bf16[2,64,128]{2,1,0:T(8,128)(2,1)S(1)}, u32[]{:S(2)}, u32[]{:S(2)}) %collective-permute-start) | collective-permute-done | bytes 32800 | tf_op jit(solution)/shard_map/ppermute | solution.py:22
  46.8 0.1 constant_dynamic-update-slice_fusion.1
  46.9 2.1 %collective-permute-done.1 = bf16[2,64,128]{2,1,0:T(8,128)(2,1)S(1)} collective-permute-done((bf16[2,64,128]{2,1,0:T(8,128)(2,1)S(1)}, bf16[2,64,128]{2,1,0:T(8,128)(2,1)S(1)}, u32[]{:S(2)}, u32[]{:S(2)}) %collective-permute-start.1) | collective-permute-done | bytes 32800 | tf_op jit(solution)/shard_map/ppermute | solution.py:25
  49.0 5.2 %collective-permute-start.2 = (bf16[36,2,128]{2,1,0:T(2,128)(2,1)S(1)}, bf16[36,2,128]{2,1,0:T(2,128)(2,1)S(1)}, u32[]{:S(2)}, u32[]{:S(2)}) collective-permute-start(bf16[36,2,128]{2,1,0:T(2,128)(2,1)S(1)} %get-tuple-element.13), channel_id=1, source_target_pairs={{0,1},{1,2},{2,3},{3,4},{4,5},{5,6},{6,7},{8,9},{9,10},{10,11},{11... | collective-permute-start | bytes 55304 | tf_op jit(solution)/shard_map/ppermute | solution.py:22
  54.2 1.9 %collective-permute-start.3 = (bf16[36,2,128]{2,1,0:T(2,128)(2,1)S(1)}, bf16[36,2,128]{2,1,0:T(2,128)(2,1)S(1)}, u32[]{:S(2)}, u32[]{:S(2)}) collective-permute-start(bf16[36,2,128]{2,1,0:T(2,128)(2,1)S(1)} %get-tuple-element.14), channel_id=1, source_target_pairs={{1,0},{2,1},{3,2},{4,3},{5,4},{6,5},{7,6},{9,8},{10,9},{11,10},{12... | collective-permute-start | bytes 55304 | tf_op jit(solution)/shard_map/ppermute | solution.py:25
  56.1 0.6 pad_maximum_fusion.weight_ref
  56.8 0.0 copy-done.3
  56.8 0.6 reshape.250.lce_ref
  57.4 61.6 %collective-permute-done.2 = bf16[36,2,128]{2,1,0:T(2,128)(2,1)S(1)} collective-permute-done((bf16[36,2,128]{2,1,0:T(2,128)(2,1)S(1)}, bf16[36,2,128]{2,1,0:T(2,128)(2,1)S(1)}, u32[]{:S(2)}, u32[]{:S(2)}) %collective-permute-start.2) | collective-permute-done | bytes 18464 | tf_op jit(solution)/shard_map/ppermute | solution.py:22
  118.9 0.0 collective-permute-done.3
  118.9 1.2 fusion.4.padded_ref
  120.1 5.9 %context.1 = (f32[2048,128]{1,0:T(8,128)}, bf16[2048,128]{1,0:T(8,128)(2,1)}) custom-call(bf16[36,80,128]{2,1,0:T(8,128)(2,1)} %fusion.4.padded_ref, f32[1,128]{1,0:T(1,128)} %bitcast.7, bf16[128,256]{1,0:T(8,128)(2,1)} %pad_maximum_fusion.weight_ref, f32[5,5,1,128]{3,2,1,0:T(1,128)} %reshape.250.lce_ref), custom_call_target="tpu_custom_call" | custom-call | flops 157286400 | bytes 2621440 | tf_op jit(solution)/shard_map/context/pallas_call | solution.py:108
  126.0 0.0 copy-done.1
  126.0 0.0 all-to-all-done.1
  126.0 21.3 %tail.1 = bf16[32,64,128]{2,1,0:T(8,128)(2,1)} custom-call(s32[128]{0:T(128)} %copy-done.4, bf16[256,64,128]{2,1,0:T(8,128)(2,1)} %bitcast.3.refs_1_.refs_2_.refs_3_.refs_4_.refs_5_.refs_6_.refs_7_.refs_8_.refs_9_.refs_10_.refs_11_.refs_12_.refs_13_.refs_14_.refs_15_.refs_16_, ...), custom_call_target="tpu_custom_call" | custom-call | flops 1048576000 | bytes 4194304 | tf_op jit(solution)/shard_map/tail/pallas_call | solution.py:239
  (7 shorter events, 0.1 us)
Async XLA Ops:
  1.1 19.1 %copy-start.4 = (s32[128]{0:T(128)}, s32[128]{0:T(128)S(1)}, u32[]{:S(2)}) copy-start(s32[128]{0:T(128)S(1)} %multiply_add_fusion.refs_0_) | copy-start | bytes 1540
  1.9 11.0 %all-to-all-start = ((s32[32,1,8]{2,1,0:T(1,128)}), s32[32,1,8]{2,1,0:T(1,128)S(1)}, u32[]{:S(2)}, u32[]{:S(2)}) async-start(s32[32,1,8]{2,1,0:T(1,128)} %bitcast), calls=%async_computation | async-start | bytes 32768 | tf_op jit(solution)/shard_map/all_to_all | solution.py:281
  20.2 6.0 %copy-start = (bf16[32,64,128]{2,1,0:T(8,128)(2,1)S(1)}, bf16[32,64,128]{2,1,0:T(8,128)(2,1)}, u32[]{:S(2)}) copy-start(bf16[32,64,128]{2,1,0:T(8,128)(2,1)} %refs_19_.1) | copy-start | bytes 1572868
  20.2 11.3 %copy-start.2 = (bf16[128,384]{1,0:T(8,128)(2,1)S(1)}, bf16[128,384]{1,0:T(8,128)(2,1)}, u32[]{:S(2)}) copy-start(bf16[128,384]{1,0:T(8,128)(2,1)} %param.12) | copy-start | bytes 294916
  20.2 105.8 %all-to-all-start.1 = ((bf16[32,8,64,128]{3,2,1,0:T(8,128)(2,1)}), bf16[32,8,64,128]{3,2,1,0:T(8,128)(2,1)}, u32[]{:S(2)}, u32[]{:S(2)}) async-start(bf16[32,8,64,128]{3,2,1,0:T(8,128)(2,1)} %bitcast.5), calls=%async_computation.1 | async-start | bytes 8388608 | tf_op jit(solution)/shard_map/all_to_all | solution.py:287
  26.2 30.6 %copy-start.3 = (f32[5,5,128]{2,1,0:T(8,128)S(1)}, f32[5,5,128]{2,1,0:T(8,128)}, u32[]{:S(2)}) copy-start(f32[5,5,128]{2,1,0:T(8,128)} %param.13) | copy-start | bytes 38404
  26.2 20.6 %collective-permute-start = (bf16[2,64,128]{2,1,0:T(8,128)(2,1)S(1)}, bf16[2,64,128]{2,1,0:T(8,128)(2,1)S(1)}, u32[]{:S(2)}, u32[]{:S(2)}) collective-permute-start(bf16[2,64,128]{2,1,0:T(8,128)(2,1)S(1)} %get-tuple-element.16), channel_id=1, source_target_pairs={{0,8},{8,16},{16,24},{1,9},{9,17},{17,25},{2,10},{10,18},{18,26},{... | collective-permute-start | bytes 98312 | tf_op jit(solution)/shard_map/ppermute | solution.py:22
  29.6 19.3 %collective-permute-start.1 = (bf16[2,64,128]{2,1,0:T(8,128)(2,1)S(1)}, bf16[2,64,128]{2,1,0:T(8,128)(2,1)S(1)}, u32[]{:S(2)}, u32[]{:S(2)}) collective-permute-start(bf16[2,64,128]{2,1,0:T(8,128)(2,1)S(1)} %get-tuple-element.15), channel_id=1, source_target_pairs={{8,0},{16,8},{24,16},{9,1},{17,9},{25,17},{10,2},{18,10},{26,18},{... | collective-permute-start | bytes 98312 | tf_op jit(solution)/shard_map/ppermute | solution.py:25
  32.2 93.8 %copy-start.1 = (bf16[128,128]{1,0:T(8,128)(2,1)}, bf16[128,128]{1,0:T(8,128)(2,1)S(1)}, u32[]{:S(2)}) copy-start(bf16[128,128]{1,0:T(8,128)(2,1)S(1)} %get-tuple-element.19.refs_21_) | copy-start | bytes 98308
  49.0 70.0 %collective-permute-start.2 = (bf16[36,2,128]{2,1,0:T(2,128)(2,1)S(1)}, bf16[36,2,128]{2,1,0:T(2,128)(2,1)S(1)}, u32[]{:S(2)}, u32[]{:S(2)}) collective-permute-start(bf16[36,2,128]{2,1,0:T(2,128)(2,1)S(1)} %get-tuple-element.13), channel_id=1, source_target_pairs={{0,1},{1,2},{2,3},{3,4},{4,5},{5,6},{6,7},{8,9},{9,10},{10,11},{11... | collective-permute-start | bytes 55304 | tf_op jit(solution)/shard_map/ppermute | solution.py:22
  54.2 64.7 %collective-permute-start.3 = (bf16[36,2,128]{2,1,0:T(2,128)(2,1)S(1)}, bf16[36,2,128]{2,1,0:T(2,128)(2,1)S(1)}, u32[]{:S(2)}, u32[]{:S(2)}) collective-permute-start(bf16[36,2,128]{2,1,0:T(2,128)(2,1)S(1)} %get-tuple-element.14), channel_id=1, source_target_pairs={{1,0},{2,1},{3,2},{4,3},{5,4},{6,5},{7,6},{9,8},{10,9},{11,10},{12... | collective-permute-start | bytes 55304 | tf_op jit(solution)/shard_map/ppermute | solution.py:25
